TPU v7x, 32 devices: a whole 2x2x4 slice. The times are simulated.
32 devices in a mesh: fsdp: 4 (over y, x), ctx: 2 (over core), tp: 4 (over z).
Axes of the slice: x: 2, y: 2, z: 4, core: 2. Of those that a mesh axis runs over, the one named last changes fastest.
Arguments:
- residual: bfloat16 [8192, 2048], P(('fsdp', 'ctx'), 'tp'), may hold values from -6 to 6
- out_grad: bfloat16 [8192, 2048], P(('fsdp', 'ctx'), 'tp'), may hold values from -6 to 6
- path_depth: int32 [8192], P(('fsdp', 'ctx')), may hold values from 0 to 895, as said below
- seg_lengths: int32 [4, 13], P('fsdp'), may hold values from 64 to 512, as said below
- parents: int32 [4, 13], P('fsdp'), may hold values from 0 to 4, as said below
- attn_norm_gain: bfloat16 [2048], P('tp'), may hold values from 0.099609375 to 1.8984375
- attn_norm_bias: bfloat16 [2048], P('tp'), may hold values from -1.5 to 1.5
- ffn_norm_gain: bfloat16 [2048], P('tp'), may hold values from 0.099609375 to 1.8984375
- ffn_norm_bias: bfloat16 [2048], P('tp'), may hold values from -1.5 to 1.5
- qkv_weight: bfloat16 [2048, 6144], P(('fsdp', 'ctx'), 'tp'), may hold values from -0.125 to 0.125
- qkv_bias: bfloat16 [6144], P('tp'), may hold values from -2.5 to 2.5
- dense_weight: bfloat16 [2048, 2048], P('tp', ('fsdp', 'ctx')), may hold values from -2 to 2
- dense_bias: bfloat16 [2048], P('tp'), may hold values from -2.5 to 2.5
- up_weight: bfloat16 [2048, 8192], P(('fsdp', 'ctx'), 'tp'), may hold values from -0.125 to 0.125
- up_bias: bfloat16 [8192], P('tp'), may hold values from -2.5 to 2.5
- down_weight: bfloat16 [8192, 2048], P('tp', ('fsdp', 'ctx')), may hold values from -0.0625 to 0.0625
- down_bias: bfloat16 [2048], P('tp'), may hold values from -2.5 to 2.5
Outputs:
- output: bfloat16 [8192, 2048], P(('fsdp', 'ctx'), 'tp')
- input_grad: bfloat16 [8192, 2048], P(('fsdp', 'ctx'), 'tp')
- grad_attn_norm_gain: float32 [2048], P('tp')
- grad_attn_norm_bias: float32 [2048], P('tp')
- grad_ffn_norm_gain: float32 [2048], P('tp')
- grad_ffn_norm_bias: float32 [2048], P('tp')
- grad_qkv_weight: float32 [2048, 6144], P(('fsdp', 'ctx'), 'tp')
- grad_qkv_bias: float32 [6144], P('tp')
- grad_dense_weight: float32 [2048, 2048], P('tp', ('fsdp', 'ctx'))
- grad_dense_bias: float32 [2048], P('tp')
- grad_up_weight: float32 [2048, 8192], P(('fsdp', 'ctx'), 'tp')
- grad_up_bias: float32 [8192], P('tp')
- grad_down_weight: float32 [8192, 2048], P('tp', ('fsdp', 'ctx'))
- grad_down_bias: float32 [2048], P('tp')
Inputs may be any that keep to these rules, and one draw needn't show every extreme that they name: `seg_lengths`: row t lists tree t's segments in order: the trunk of 512 tokens, 4 branches, then 8 leaves; each row sums to 2048. `parents`: entry s of row t is the segment that segment s hangs from: 0 for the trunk itself and for each branch, a branch for each leaf; each branch holds exactly two leaves. `path_depth`: A token's place within its segment plus the lengths of the segment's proper ancestors in its tree.
All inputs are finite; a program needn't handle non-finite values.
Results may differ from a plain program's by a relative error of at most 0.012.
Values may be sent and summed in bfloat16 or wider, within the bound.
No kernel may reach another device: no remote copies, remote signals or barrier semaphores. Data moves between devices by JAX's collectives and lax.ppermute only.
A program may use at most 256 MiB of HBM per device.

v0:
```python
from functools import partial
import math
import jax
import jax.numpy as jnp
from jax import lax
from jax.sharding import PartitionSpec as P

HEAD_DIM = 256
ROTARY = 64
SEGS = 13
norm_epsilon = 1e-05
masked_score = -1e30
block_limit = 512


def from_behind(x, axis, by):
    peers = lax.axis_size(axis)
    pairs = [(i, i + by) for i in range(peers) if 0 <= i + by < peers]
    return lax.ppermute(x, axis, pairs)


def rotary(vectors, places):
    half_rot = ROTARY // 2
    frequency = jnp.power(10000.0, -2.0 * jnp.arange(half_rot).astype(jnp.float32) / ROTARY)
    angles = places.astype(jnp.float32)[:, None] * frequency[None, :]
    cosine = jnp.cos(angles)[:, None, :]
    sine_part = jnp.sin(angles)[:, None, :]
    first_half = vectors[..., :half_rot]
    second_half = vectors[..., half_rot:ROTARY]
    return jnp.concatenate(
        [
            first_half * cosine - second_half * sine_part,
            second_half * cosine + first_half * sine_part,
            vectors[..., ROTARY:],
        ],
        axis=-1,
    )


def tree_tables(lengths, parent):
    starts = jnp.cumsum(lengths) - lengths
    labels = jnp.arange(SEGS)
    grand_parent = jnp.sum(
        jnp.where(parent[:, None] == labels[None, :], parent[None, :], 0), axis=1
    )
    ancestor = (
        (labels[None, :] == labels[:, None])
        | (labels[None, :] == parent[:, None])
        | (labels[None, :] == grand_parent[:, None])
    )
    return (starts, ancestor.astype(jnp.float32))


def segment_onehot(places, starts):
    membership = jnp.sum((places[:, None] >= starts[None, :]).astype(jnp.int32), axis=1) - 1
    return (membership[:, None] == jnp.arange(SEGS)[None, :]).astype(jnp.float32)


def visible(hot_query, place_query, hot_key, place_key, ancestor):
    reachable = jnp.dot(jnp.dot(hot_query, ancestor), hot_key.T)
    return (reachable > 0.5) & (place_key[None, :] <= place_query[:, None])


def on_device(
    residual,
    out_grad,
    path_depth,
    seg_lengths,
    parents,
    attn_norm_gain,
    attn_norm_bias,
    ffn_norm_gain,
    ffn_norm_bias,
    qkv_weight,
    qkv_bias,
    dense_weight,
    dense_bias,
    up_weight,
    up_bias,
    down_weight,
    down_bias,
):
    row_count = residual.shape[0]
    local_width = residual.shape[1]
    head_count = qkv_weight.shape[1] // (3 * HEAD_DIM)
    score_scale = 1.0 / math.sqrt(HEAD_DIM)
    ctx_index = lax.axis_index("ctx")
    tp_index = lax.axis_index("tp")
    norm_stack = jnp.stack([attn_norm_gain, attn_norm_bias, ffn_norm_gain, ffn_norm_bias])
    full_rows, norm_terms = (
        lax.all_gather(residual, "tp", axis=1, tiled=True),
        lax.all_gather(norm_stack, "tp", axis=1, tiled=True),
    )
    norm_terms = norm_terms.astype(jnp.float32)
    qkv_full, up_full = (
        lax.all_gather(qkv_weight, ("fsdp", "ctx"), axis=0, tiled=True),
        lax.all_gather(up_weight, ("fsdp", "ctx"), axis=0, tiled=True),
    )
    dense_full, down_full = (
        lax.all_gather(dense_weight, ("fsdp", "ctx"), axis=1, tiled=True),
        lax.all_gather(down_weight, ("fsdp", "ctx"), axis=1, tiled=True),
    )
    rows_wide = full_rows.astype(jnp.float32)
    centred = rows_wide - jnp.mean(rows_wide, axis=1, keepdims=True)
    inverse_scale = lax.rsqrt(jnp.mean(centred * centred, axis=1, keepdims=True) + norm_epsilon)
    normed = centred * inverse_scale
    attn_in = (normed * norm_terms[0] + norm_terms[1]).astype(jnp.bfloat16)
    ffn_in = (normed * norm_terms[2] + norm_terms[3]).astype(jnp.bfloat16)
    joined = (
        jnp.dot(attn_in, qkv_full, preferred_element_type=jnp.float32)
        + qkv_bias.astype(jnp.float32)
    ).reshape(row_count, head_count, 3, HEAD_DIM)
    queries_pre = joined[:, :, 0]
    query_rows = rotary(queries_pre, path_depth).astype(jnp.bfloat16)
    key_rows = rotary(joined[:, :, 1], path_depth).astype(jnp.bfloat16)
    value_rows = joined[:, :, 2].astype(jnp.bfloat16)
    far_keys, far_values = from_behind((key_rows, value_rows), "ctx", 1)
    starts, ancestor = tree_tables(seg_lengths[0], parents[0])
    places = ctx_index * row_count + jnp.arange(row_count, dtype=jnp.int32)
    key_places = jnp.concatenate([places - row_count, places])
    hot_query = segment_onehot(places, starts)
    hot_key = segment_onehot(key_places, starts)
    all_keys = jnp.concatenate([far_keys, key_rows], axis=0)
    all_values = jnp.concatenate([far_values, value_rows], axis=0)
    block_starts = list(range(0, row_count, block_limit))

    def block_scores(block_start, block_size, key_set):
        key_span = row_count + block_start + block_size
        query_block = query_rows[block_start : block_start + block_size]
        scores = (
            jnp.einsum(
                "nhe,lhe->hnl", query_block, key_set[:key_span], preferred_element_type=jnp.float32
            )
            * score_scale
        )
        reachable = visible(
            hot_query[block_start : block_start + block_size],
            places[block_start : block_start + block_size],
            hot_key[:key_span],
            key_places[:key_span],
            ancestor,
        )
        return jnp.where(reachable[None], scores, masked_score)

    out_blocks = []
    log_totals = []
    for block_start in block_starts:
        block_size = min(block_limit, row_count - block_start)
        key_span = row_count + block_start + block_size
        scores = block_scores(block_start, block_size, all_keys)
        row_top = jnp.max(scores, axis=-1, keepdims=True)
        exp_scores = jnp.exp(scores - row_top)
        exp_total = jnp.sum(exp_scores, axis=-1, keepdims=True)
        attn_probs = exp_scores / exp_total
        out_blocks.append(
            jnp.einsum(
                "hnl,lhe->nhe",
                attn_probs.astype(jnp.bfloat16),
                all_values[:key_span],
                preferred_element_type=jnp.float32,
            )
        )
        log_totals.append(row_top + jnp.log(exp_total))
    attended = (
        jnp.concatenate(out_blocks, axis=0)
        .reshape(row_count, head_count * HEAD_DIM)
        .astype(jnp.bfloat16)
    )
    hidden_pre = jnp.dot(ffn_in, up_full, preferred_element_type=jnp.float32) + up_bias.astype(
        jnp.float32
    )
    hidden_wide, gelu_back = jax.vjp(partial(jax.nn.gelu, approximate=False), hidden_pre)
    hidden = hidden_wide.astype(jnp.bfloat16)
    partial_out = jnp.dot(attended, dense_full, preferred_element_type=jnp.float32) + jnp.dot(
        hidden, down_full, preferred_element_type=jnp.float32
    )
    shared_out = lax.psum_scatter(partial_out, "tp", scatter_dimension=1, tiled=True)
    output = (
        residual.astype(jnp.float32)
        + shared_out
        + dense_bias.astype(jnp.float32)
        + down_bias.astype(jnp.float32)
    ).astype(jnp.bfloat16)
    cotangent = lax.all_gather(out_grad, "tp", axis=1, tiled=True)
    grad_out_bias = jnp.sum(out_grad.astype(jnp.float32), axis=0)
    grad_dense_w = jnp.einsum("rf,rd->fd", attended, cotangent, preferred_element_type=jnp.float32)
    grad_down_w = jnp.einsum("rf,rd->fd", hidden, cotangent, preferred_element_type=jnp.float32)
    grad_attended = jnp.einsum(
        "rd,fd->rf", cotangent, dense_full, preferred_element_type=jnp.float32
    ).astype(jnp.bfloat16)
    grad_hidden = jnp.einsum("rd,fd->rf", cotangent, down_full, preferred_element_type=jnp.float32)
    grad_pre = gelu_back(grad_hidden)[0].astype(jnp.bfloat16)
    grad_up_w = jnp.einsum("rd,rf->df", ffn_in, grad_pre, preferred_element_type=jnp.float32)
    grad_up_b = jnp.sum(grad_pre.astype(jnp.float32), axis=0)
    grad_ffn_in = jnp.einsum("rf,df->rd", grad_pre, up_full, preferred_element_type=jnp.float32)
    key_set = all_keys
    grad_att_heads = grad_attended.reshape(row_count, head_count, HEAD_DIM)
    grad_query_parts = []
    grad_key_all = jnp.zeros((2 * row_count, head_count, HEAD_DIM), jnp.float32)
    grad_value_all = jnp.zeros((2 * row_count, head_count, HEAD_DIM), jnp.float32)
    for block_number, block_start in enumerate(block_starts):
        block_size = min(block_limit, row_count - block_start)
        key_span = row_count + block_start + block_size
        scores = block_scores(block_start, block_size, key_set)
        attn_probs = jnp.exp(scores - log_totals[block_number])
        grad_block = grad_att_heads[block_start : block_start + block_size]
        grad_value_all = grad_value_all.at[:key_span].add(
            jnp.einsum(
                "hnl,nhe->lhe",
                attn_probs.astype(jnp.bfloat16),
                grad_block,
                preferred_element_type=jnp.float32,
            )
        )
        grad_dots = jnp.einsum(
            "nhe,lhe->hnl", grad_block, all_values[:key_span], preferred_element_type=jnp.float32
        )
        row_delta = jnp.sum(attn_probs * grad_dots, axis=-1, keepdims=True)
        grad_scores = (attn_probs * (grad_dots - row_delta)).astype(jnp.bfloat16)
        grad_query_parts.append(
            jnp.einsum(
                "hnl,lhe->nhe", grad_scores, key_set[:key_span], preferred_element_type=jnp.float32
            )
            * score_scale
        )
        grad_key_all = grad_key_all.at[:key_span].add(
            jnp.einsum(
                "hnl,nhe->lhe",
                grad_scores,
                query_rows[block_start : block_start + block_size],
                preferred_element_type=jnp.float32,
            )
            * score_scale
        )
    arriving_keys, arriving_values = from_behind(
        (grad_key_all[:row_count], grad_value_all[:row_count]), "ctx", -1
    )
    grad_keys = grad_key_all[row_count:] + arriving_keys
    grad_values = grad_value_all[row_count:] + arriving_values
    grad_queries = jnp.concatenate(grad_query_parts, axis=0)
    rotated_unused, rotary_back = jax.vjp(lambda vectors: rotary(vectors, path_depth), queries_pre)
    grad_joined = (
        jnp.stack([rotary_back(grad_queries)[0], rotary_back(grad_keys)[0], grad_values], axis=2)
        .astype(jnp.bfloat16)
        .reshape(row_count, head_count * 3 * HEAD_DIM)
    )
    grad_qkv_w = jnp.einsum("rd,rf->df", attn_in, grad_joined, preferred_element_type=jnp.float32)
    grad_qkv_b = jnp.sum(grad_joined.astype(jnp.float32), axis=0)
    grad_attn_in = jnp.einsum(
        "rf,df->rd", grad_joined, qkv_full, preferred_element_type=jnp.float32
    )
    total_attn, total_ffn = lax.psum((grad_attn_in, grad_ffn_in), "tp")

    def norm_back(total_grad, gain_row):
        scaled = total_grad * gain_row
        mean_plain = jnp.mean(scaled, axis=1, keepdims=True)
        mean_normed = jnp.mean(scaled * normed, axis=1, keepdims=True)
        back_rows = inverse_scale * (scaled - mean_plain - normed * mean_normed)
        gain_grad = jnp.sum(total_grad * normed, axis=0)
        shift_grad = jnp.sum(total_grad, axis=0)
        return (
            lax.dynamic_slice_in_dim(back_rows, tp_index * local_width, local_width, 1),
            lax.dynamic_slice_in_dim(gain_grad, tp_index * local_width, local_width, 0),
            lax.dynamic_slice_in_dim(shift_grad, tp_index * local_width, local_width, 0),
        )

    back_attn, attn_gain_grad, attn_shift_grad = norm_back(total_attn, norm_terms[0])
    back_ffn, ffn_gain_grad, ffn_shift_grad = norm_back(total_ffn, norm_terms[2])
    norm_grads = jnp.stack([attn_gain_grad, attn_shift_grad, ffn_gain_grad, ffn_shift_grad])
    back_total = back_attn + back_ffn
    input_grad = (out_grad.astype(jnp.float32) + back_total).astype(jnp.bfloat16)
    qkv_bias_grad, up_bias_grad, out_bias_grad, norm_totals = lax.psum(
        (grad_qkv_b, grad_up_b, grad_out_bias, norm_grads), ("fsdp", "ctx")
    )
    qkv_weight_grad, up_weight_grad = (
        lax.psum_scatter(
            grad_qkv_w.astype(jnp.bfloat16), ("fsdp", "ctx"), scatter_dimension=0, tiled=True
        ).astype(jnp.float32),
        lax.psum_scatter(
            grad_up_w.astype(jnp.bfloat16), ("fsdp", "ctx"), scatter_dimension=0, tiled=True
        ).astype(jnp.float32),
    )
    dense_weight_grad, down_weight_grad = (
        lax.psum_scatter(
            grad_dense_w.astype(jnp.bfloat16), ("fsdp", "ctx"), scatter_dimension=1, tiled=True
        ).astype(jnp.float32),
        lax.psum_scatter(
            grad_down_w.astype(jnp.bfloat16), ("fsdp", "ctx"), scatter_dimension=1, tiled=True
        ).astype(jnp.float32),
    )
    return (
        output,
        input_grad,
        norm_totals[0],
        norm_totals[1],
        norm_totals[2],
        norm_totals[3],
        qkv_weight_grad,
        qkv_bias_grad,
        dense_weight_grad,
        out_bias_grad,
        up_weight_grad,
        up_bias_grad,
        down_weight_grad,
        out_bias_grad,
    )


def solution(mesh):
    placed = (
        P(("fsdp", "ctx"), "tp"),
        P(("fsdp", "ctx"), "tp"),
        P(("fsdp", "ctx")),
        P("fsdp", None),
        P("fsdp", None),
        P("tp"),
        P("tp"),
        P("tp"),
        P("tp"),
        P(("fsdp", "ctx"), "tp"),
        P("tp"),
        P("tp", ("fsdp", "ctx")),
        P("tp"),
        P(("fsdp", "ctx"), "tp"),
        P("tp"),
        P("tp", ("fsdp", "ctx")),
        P("tp"),
    )
    return jax.shard_map(
        on_device,
        mesh=mesh,
        in_specs=placed,
        out_specs=(
            P(("fsdp", "ctx"), "tp"),
            P(("fsdp", "ctx"), "tp"),
            P("tp"),
            P("tp"),
            P("tp"),
            P("tp"),
            P(("fsdp", "ctx"), "tp"),
            P("tp"),
            P("tp", ("fsdp", "ctx")),
            P("tp"),
            P(("fsdp", "ctx"), "tp"),
            P("tp"),
            P("tp", ("fsdp", "ctx")),
            P("tp"),
        ),
        check_vma=False,
    )
```

profile of v0, /device:TPU:0, one launch (start us, length us, event | category | flops | bytes accessed | tf_op | source)
XLA Modules:
  0.0 1348.0 jit_solution(2497140615921052916)
XLA Ops:
  19.3 15.1 %all_gather.22 = bf16[4,2048]{1,0:T(4,128)(2,1)S(1)} all-gather(bf16[4,512]{1,0:T(4,128)(2,1)S(1)} %pad_maximum_fusion.16), channel_id=1, replica_groups=mesh['fsdp'=4,'ctx'=2,'tp'=4] {'tp'}, dimensions={1}, use_global_device_ids=true | all-gather | bytes 20480 | tf_op jit(solution)/shard_map/all_gather | solution.py:92
  42.4 50.9 %all-gather.7.cloned.1.call-done = bf16[1024,2048]{1,0:T(8,128)(2,1)} async-done(((bf16[1024,512]{1,0:T(8,128)(2,1)}), bf16[1024,2048]{1,0:T(8,128)(2,1)}) %all-gather.7.cloned.1.call-update) | async-done | bytes 4194320 | tf_op jit(solution)/shard_map/all_gather | solution.py:91
  98.0 41.3 %all-gather.9.cloned.1.call-done = bf16[2048,1536]{1,0:T(8,128)(2,1)} async-done(((bf16[256,1536]{1,0:T(8,128)(2,1)}), bf16[2048,1536]{1,0:T(8,128)(2,1)}) %all-gather.9.cloned.1.call-update) | async-done | bytes 6291472 | tf_op jit(solution)/shard_map/all_gather | solution.py:96
  139.3 12.4 convolution_add_fusion
  151.7 6.6 copy.87
  158.3 5.1 fusion.69
  169.0 3.3 subtract_convert_fusion
  174.2 3.3 collective-permute-start.1
  177.5 74.1 %all-gather.17.cloned.1.call-done = bf16[1024,2048]{1,0:T(8,128)(2,1)} async-done(((bf16[1024,512]{1,0:T(8,128)(2,1)}), bf16[1024,2048]{1,0:T(8,128)(2,1)}) %all-gather.17.cloned.1.call-update) | async-done | bytes 4194320 | tf_op jit(solution)/shard_map/all_gather | solution.py:184
  251.6 5.2 convolution_convert_fusion.4
  262.7 3.5 fusion.75
  267.4 4.0 fusion.74
  292.9 5.3 bitcast_add_fusion.1
  308.3 3.7 convolution_convert_fusion.3
  328.7 3.1 copy.105
  331.8 13.6 %convolution_convert_fusion.2 = bf16[2048,1536]{1,0:T(8,128)(2,1)} fusion(bf16[1024,1536]{0,1:T(8,128)(2,1)} %bitcast.86, bf16[1024,2048]{1,0:T(8,128)(2,1)} %all-gather.7.cloned.1.call-done, f32[2048]{0:T(1024)S(1)} %bitcast.101, f32[2048]{0:T(1024)S(1)} %bitcast.89, f32[1024]{0:T(1024)S(1)} %add_rsqrt_fusion, f32[1024]{0:T(1024)S(1)} %broadcast_multiply_fusion.6), kind=kOutput, calls=%fused_computation.37 | convolution fusion | flops 6458179584 | bytes 13656064 | tf_op jit(solution)/shard_map/rd,rf->df/dot_general | solution.py:247
  346.1 14.9 %fusion.65 = f32[1024,2048]{1,0:T(8,128)} fusion(bf16[2048,2048]{1,0:T(8,128)(2,1)} %all-gather.13.cloned.1.call-done, bf16[1024,2048]{1,0:T(8,128)(2,1)} %all-gather.7.cloned.1.call-done, f32[2048]{0:T(1024)S(1)} %bitcast.98, f32[2048]{0:T(1024)S(1)} %bitcast.91, f32[1024]{0:T(1024)S(1)} %add_rsqrt_fusion, f32[1024]{0:T(1024)S(1)} %broadcast_multiply_fusion.6), kind=kOutput, calls=%fused_computation.166 | convolution fusion | flops 8602517504 | bytes 20996096 | tf_op jit(solution)/shard_map/dot_general | solution.py:169
  360.9 5.1 all-gather.15.cloned.1.call-done
  366.0 33.7 %convert_reduce_fusion.1 = (f32[2048]{0:T(1024)S(1)}, bf16[1024,2048]{1,0:T(8,128)(2,1)}, f32[1024,2048]{1,0:T(8,128)}) fusion(f32[1024,2048]{1,0:T(8,128)} %fusion.65, f32[2048]{0:T(1024)S(1)} %copy-done.36, bf16[1024,2048]{1,0:T(8,128)(2,1)} %all-gather.17.cloned.1.call-done, bf16[2048,2048]{1,0:T(8,128)(2,1)} %all-gather.15.cloned.1.call-done), kind=kOutput, calls=%fused_computation.7 | convolution fusion | flops 8747218944 | bytes 33570816 | tf_op jit(solution)/shard_map/rd,fd->rf/dot_general | solution.py:191
  399.8 8.2 multiply_convert_fusion.1
  410.0 13.6 %convolution_convert_fusion = bf16[2048,2048]{1,0:T(8,128)(2,1)} fusion(bf16[1024,2048]{1,0:T(8,128)(2,1)S(1)} %multiply_convert_fusion.1, bf16[1024,2048]{1,0:T(8,128)(2,1)} %all-gather.17.cloned.1.call-done), kind=kOutput, calls=%fused_computation.35 | convolution fusion | flops 8594128896 | bytes 16777216 | tf_op jit(solution)/shard_map/rf,rd->fd/dot_general | solution.py:187
  423.6 15.9 %convolution_convert_fusion.1 = bf16[2048,2048]{1,0:T(8,128)(2,1)} fusion(bf16[1024,2048]{1,0:T(8,128)(2,1)} %get-tuple-element.97, bf16[1024,2048]{1,0:T(8,128)(2,1)} %all-gather.7.cloned.1.call-done, f32[2048]{0:T(1024)S(1)} %bitcast.99, f32[2048]{0:T(1024)S(1)} %bitcast.92, f32[1024]{0:T(1024)S(1)} %add_rsqrt_fusion, f32[1024]{0:T(1024)S(1)} %broadcast_multiply_fusion.6), kind=kOutput, calls=%fused_computation.36 | convolution fusion | flops 8606711808 | bytes 16801792 | tf_op jit(solution)/shard_map/rd,rf->df/dot_general | solution.py:193
  441.4 11.2 fusion.77
  452.7 13.4 fusion.78
  466.1 12.8 fusion.76
  479.0 5.9 convolution_add_fusion.1
  490.0 60.8 %reduce-scatter.14.cloned.1.call-done = bf16[2048,256]{1,0:T(8,128)(2,1)} async-done(((bf16[2048,2048]{1,0:T(8,128)(2,1)}), bf16[2048,256]{1,0:T(8,128)(2,1)}) %reduce-scatter.14.cloned.1.call-update) | async-done | bytes 1048592 | tf_op jit(solution)/shard_map/reduce_scatter | solution.py:287
  553.5 72.3 %reduce-scatter.12.cloned.1.call-done = bf16[256,2048]{1,0:T(8,128)(2,1)} async-done(((bf16[2048,2048]{1,0:T(8,128)(2,1)}), bf16[256,2048]{1,0:T(8,128)(2,1)}) %reduce-scatter.12.cloned.1.call-update) | async-done | bytes 1048592 | tf_op jit(solution)/shard_map/reduce_scatter | solution.py:279
  628.6 563.1 %all-reduce.12.cloned.1.call-done = (f32[1024,2048]{1,0:T(8,128)}, f32[1024,2048]{1,0:T(8,128)}) async-done(((f32[1024,2048]{1,0:T(8,128)}, f32[1024,2048]{1,0:T(8,128)}), (f32[1024,2048]{1,0:T(8,128)}, f32[1024,2048]{1,0:T(8,128)})) %all-reduce.12.cloned.1.call-update) | async-done | bytes 16777232 | tf_op jit(solution)/shard_map/psum | solution.py:252
  1191.8 11.7 fusion.66
  1205.8 26.3 %all-reduce.8 = (f32[4,512]{1,0:T(4,128)S(1)}, f32[1536]{0:T(1024)}, f32[512]{0:T(512)S(1)}, f32[2048]{0:T(1024)}) all-reduce(f32[4,512]{1,0:T(4,128)S(1)} %pad_maximum_fusion.15, f32[1536]{0:T(1024)S(1)} %reduce_sum.200, f32[512]{0:T(512)S(1)} %get-tuple-element.121, ...), channel_id=1, replica_groups=mesh['fsdp'=4,'ctx'=2,'tp'=4] {'fsdp','ctx'}, use_global_device_ids=true, to_apply=%region_23.24 | all-reduce | flops 6144 | bytes 49152 | tf_op jit(solution)/shard_map/psum | solution.py:272
  1232.7 104.7 %reduce-scatter.6.cloned.1.call-done = f32[1024,512]{1,0:T(8,128)} async-done(((f32[1024,2048]{1,0:T(8,128)}), f32[1024,512]{1,0:T(8,128)}) %reduce-scatter.6.cloned.1.call-update) | async-done | bytes 2097168 | tf_op jit(solution)/shard_map/reduce_scatter | solution.py:177
  (220 shorter events, 108.6 us)
Async XLA Ops:
  7.2 30.3 %copy-start.46 = (s32[1,13]{1,0:T(1,128)S(1)}, s32[1,13]{1,0:T(1,128)}, u32[]{:S(2)}) copy-start(s32[1,13]{1,0:T(1,128)} %param.33) | copy-start | bytes 160
  7.2 86.1 %all-gather.7.cloned.1.call-start = ((), (), s32[]{:S(2)}) async-start(), calls=%async_computation.5 | async-start | bytes 5242880 | tf_op jit(solution)/shard_map/all_gather | solution.py:91
  7.9 131.4 %all-gather.9.cloned.1.call-start = ((), (), s32[]{:S(2)}) async-start(), calls=%async_computation.6 | async-start | bytes 7077888 | tf_op jit(solution)/shard_map/all_gather | solution.py:96
  8.7 168.8 %all-gather.11.cloned.1.call-start = ((), (), s32[]{:S(2)}) async-start(), calls=%async_computation.7 | async-start | bytes 2359296 | tf_op jit(solution)/shard_map/all_gather | solution.py:100
  9.4 242.2 %all-gather.17.cloned.1.call-start = ((), (), s32[]{:S(2)}) async-start(), calls=%async_computation.11 | async-start | bytes 5242880 | tf_op jit(solution)/shard_map/all_gather | solution.py:184
  10.0 335.5 %all-gather.13.cloned.1.call-start = ((), (), s32[]{:S(2)}) async-start(), calls=%async_computation.8 | async-start | bytes 9437184 | tf_op jit(solution)/shard_map/all_gather | solution.py:97
  10.6 355.4 %all-gather.15.cloned.1.call-start = ((), (), s32[]{:S(2)}) async-start(), calls=%async_computation.9 | async-start | bytes 9437184 | tf_op jit(solution)/shard_map/all_gather | solution.py:101
  11.1 474.5 %reduce-scatter.10.cloned.1.call-start = ((), (), s32[]{:S(2)}) async-start(), calls=%async_computation.13 | async-start | bytes 2359296 | tf_op jit(solution)/shard_map/reduce_scatter | solution.py:284
  35.0 296.7 %copy-start.37 = (f32[1,2048]{1,0:T(1,128)}, f32[1,2048]{1,0:T(1,128)S(1)}, u32[]{:S(2)}) copy-start(f32[1,2048]{1,0:T(1,128)S(1)} %get-tuple-element.129) | copy-start | bytes 24580
  37.5 131.5 %copy-start.12 = (f32[1024,32]{1,0:T(8,128)}, f32[1024,32]{1,0:T(8,128)S(1)}, u32[]{:S(2)}) copy-start(f32[1024,32]{1,0:T(8,128)S(1)} %get-tuple-element.137) | copy-start | bytes 393220
  37.5 131.5 %copy-start.14 = (f32[1024,32]{1,0:T(8,128)}, f32[1024,32]{1,0:T(8,128)S(1)}, u32[]{:S(2)}) copy-start(f32[1024,32]{1,0:T(8,128)S(1)} %get-tuple-element.138) | copy-start | bytes 393220
  174.2 88.4 %collective-permute-start.1 = (bf16[1024,2,256]{2,0,1:T(8,128)(2,1)}, bf16[1024,2,256]{2,0,1:T(8,128)(2,1)}, u32[]{:S(2)}, u32[]{:S(2)}) collective-permute-start(bf16[1024,2,256]{2,0,1:T(8,128)(2,1)} %pad_maximum_fusion.11), channel_id=1, source_target_pairs={{0,4},{1,5},{2,6},{3,7},{8,12},{9,13},{10,14},{11,15},{16,20},{17,... | collective-permute-start | bytes 3145736 | tf_op jit(solution)/shard_map/ppermute | solution.py:19
  259.8 20.7 %collective-permute-start = (bf16[1024,2,256]{0,2,1:T(8,128)(2,1)S(1)}, bf16[1024,2,256]{0,2,1:T(8,128)(2,1)S(1)}, u32[]{:S(2)}, u32[]{:S(2)}) collective-permute-start(bf16[1024,2,256]{0,2,1:T(8,128)(2,1)S(1)} %fusion.42), channel_id=1, source_target_pairs={{0,4},{1,5},{2,6},{3,7},{8,12},{9,13},{10,14},{11,15},{16,20},{17,... | collective-permute-start | bytes 3145736 | tf_op jit(solution)/shard_map/ppermute | solution.py:19
  262.6 21.3 %copy-start.22 = (bf16[1024,2,256]{2,0,1:T(8,128)(2,1)}, bf16[1024,2,256]{2,0,1:T(8,128)(2,1)S(1)}, u32[]{:S(2)}) copy-start(bf16[1024,2,256]{2,0,1:T(8,128)(2,1)S(1)} %pad_maximum_fusion.10) | copy-start | bytes 3145732
  278.8 46.6 %collective-permute-start.3 = (f32[1024,2,256]{2,0,1:T(8,128)}, f32[1024,2,256]{2,0,1:T(8,128)}, u32[]{:S(2)}, u32[]{:S(2)}) collective-permute-start(f32[1024,2,256]{2,0,1:T(8,128)} %slice.263), channel_id=1, source_target_pairs={{4,0},{5,1},{6,2},{7,3},{12,8},{13,9},{14,10},{15,11},{20,16},{21,... | collective-permute-start | bytes 6291464 | tf_op jit(solution)/shard_map/ppermute | solution.py:19
  280.5 8.1 copy-start.24
  292.9 8.8 copy-start.1
  292.9 10.0 copy-start.25
  301.7 17.4 %collective-permute-start.2 = (f32[1024,2,256]{2,0,1:T(8,128)}, f32[1024,2,256]{2,0,1:T(8,128)}, u32[]{:S(2)}, u32[]{:S(2)}) collective-permute-start(f32[1024,2,256]{2,0,1:T(8,128)} %slice.261), channel_id=1, source_target_pairs={{4,0},{5,1},{6,2},{7,3},{12,8},{13,9},{14,10},{15,11},{20,16},{21,... | collective-permute-start | bytes 6291464 | tf_op jit(solution)/shard_map/ppermute | solution.py:19
  312.0 175.4 %reduce-scatter.8.cloned.1.call-start = ((), (), s32[]{:S(2)}) async-start(), calls=%async_computation.12 | async-start | bytes 7077888 | tf_op jit(solution)/shard_map/reduce_scatter | solution.py:276
  345.4 205.4 %reduce-scatter.14.cloned.1.call-start = ((), (), s32[]{:S(2)}) async-start(), calls=%async_computation.15 | async-start | bytes 9437184 | tf_op jit(solution)/shard_map/reduce_scatter | solution.py:287
  346.1 19.9 %copy-start.36 = (f32[2048]{0:T(1024)S(1)}, f32[2048]{0:T(1024)}, u32[]{:S(2)}) copy-start(f32[2048]{0:T(1024)} %convert_element_type.150) | copy-start | bytes 24580
  423.6 202.2 %reduce-scatter.12.cloned.1.call-start = ((), (), s32[]{:S(2)}) async-start(), calls=%async_computation.14 | async-start | bytes 9437184 | tf_op jit(solution)/shard_map/reduce_scatter | solution.py:279
  439.6 752.2 %all-reduce.12.cloned.1.call-start = ((), (), s32[]{:S(2)}) async-start(), calls=%async_computation.16 | async-start | bytes 33554432 | tf_op jit(solution)/shard_map/psum | solution.py:252
  441.4 11.2 copy-start.49
  466.0 12.9 copy-start.11
  466.1 12.9 copy-start.35
  466.1 871.4 %reduce-scatter.6.cloned.1.call-start = ((), (), s32[]{:S(2)}) async-start(), calls=%async_computation.10 | async-start | bytes 10485760 | tf_op jit(solution)/shard_map/reduce_scatter | solution.py:177
  484.9 706.9 %copy-start.38 = (f32[1,2048]{1,0:T(1,128)S(1)}, f32[1,2048]{1,0:T(1,128)}, u32[]{:S(2)}) copy-start(f32[1,2048]{1,0:T(1,128)} %copy-done.37) | copy-start | bytes 24580
  1191.8 12.1 copy-start.17
  1203.5 134.0 %copy-start.18 = (bf16[1024,512]{1,0:T(8,128)(2,1)S(1)}, bf16[1024,512]{1,0:T(8,128)(2,1)}, u32[]{:S(2)}) copy-start(bf16[1024,512]{1,0:T(8,128)(2,1)} %param.29) | copy-start | bytes 3145732
  1232.1 108.9 %copy-start.42 = (f32[512]{0:T(512)}, f32[512]{0:T(512)S(1)}, u32[]{:S(2)}) copy-start(f32[512]{0:T(512)S(1)} %get-tuple-element.178) | copy-start | bytes 6148
  (34 other events, 96.3 us)
Sparse Core Ops, SparseCore 0:
  9.6 83.6 all-gather.6
  95.1 44.1 all-gather.8
  141.2 28.1 all-gather.10
  170.8 80.7 all-gather.16
  253.4 52.9 all-gather.12
  308.1 57.9 all-gather.14
  369.3 41.2 reduce-scatter.9
  414.3 61.7 reduce-scatter.7
  479.5 71.2 reduce-scatter.13
  554.5 71.2 reduce-scatter.11
  628.5 563.2 all-reduce.11
  1194.0 143.4 reduce-scatter.5
where the time goes:
time: 1350 us
  waiting for transfers between devices  976 us (72%)
  matrix products  195 us (14%)
  other arithmetic  68.2 us (5%)
  local copies, waits for them, and re-layouts  42.9 us (3%)
  blocking collectives  41.4 us (3%)
  between operations  15.3 us (1%)
    psum x1, waiting for transfers between devices, on_device(): total_attn, total_ffn = lax.psum((grad_attn_in, grad_ffn_in), 'tp')  563 us
    reduce_scatter x1, waiting for transfers between devices, on_device(): lax.psum_scatter(partial_out, 'tp', scatter_dimension=1, tiled=True)  105 us
    all_gather x1, waiting for transfers between devices, on_device(): cotangent = lax.all_gather(out_grad, 'tp', axis=1, tiled=True)  74.1 us
    reduce_scatter x1, waiting for transfers between devices, on_device(): lax.psum_scatter(grad_up_w.astype(jnp.bfloat16), ('fsdp', 'ctx'), scatter...  72.3 us
    reduce_scatter x1, waiting for transfers between devices, on_device(): lax.psum_scatter(grad_down_w.astype(jnp.bfloat16), ('fsdp', 'ctx'), scatt...  60.8 us
    all_gather x1, waiting for transfers between devices, on_device(): lax.all_gather(residual, 'tp', axis=1, tiled=True)  50.9 us
    all_gather x1, waiting for transfers between devices, on_device(): lax.all_gather(qkv_weight, ('fsdp', 'ctx'), axis=0, tiled=True)  41.3 us
    dot_general x1, matrix products, on_device(): jnp.einsum('rd,fd->rf', cotangent, down_full, preferred_element_type=jnp....  33.7 us
  transfers between devices with their start and end apart: 16, of which 8 were waited for; matrix products, arithmetic and copies ran while one was open for 22% of the time, Pallas kernels for 0%

commit v1 on v0

--- a/solution.py
+++ b/solution.py
@@ -1,9 +1,11 @@
+import functools
 from functools import partial
 import math
 import jax
 import jax.numpy as jnp
 from jax import lax
 from jax.sharding import PartitionSpec as P
+from jax.lax import axis_index, axis_size, ppermute
 
 HEAD_DIM = 256
 ROTARY = 64
@@ -11,6 +13,23 @@
 norm_epsilon = 1e-05
 masked_score = -1e30
 block_limit = 512
+
+
+def wrap_targets(w_in, dim_at):
+    size_here = axis_size("tp")
+    current_block = sorted(((at, (at + 1) % size_here) for at in range(size_here)))
+    heard = w_in
+    xs_all = [heard]
+    for no in range(1, size_here):
+        heard = ppermute(heard, "tp", current_block)
+        xs_all.insert(0, heard)
+    parts_out = jnp.concatenate(xs_all, axis=dim_at)
+    tile_out = axis_index("tp") + 1
+    side_arr = jnp.roll(parts_out, shift=tile_out * w_in.shape[dim_at], axis=dim_at)
+    return side_arr
+
+
+clusters_order = functools.partial(wrap_targets, dim_at=1)
 
 
 def from_behind(x, axis, by):
@@ -181,7 +200,7 @@
         + dense_bias.astype(jnp.float32)
         + down_bias.astype(jnp.float32)
     ).astype(jnp.bfloat16)
-    cotangent = lax.all_gather(out_grad, "tp", axis=1, tiled=True)
+    cotangent = clusters_order(out_grad)
     grad_out_bias = jnp.sum(out_grad.astype(jnp.float32), axis=0)
     grad_dense_w = jnp.einsum("rf,rd->fd", attended, cotangent, preferred_element_type=jnp.float32)
     grad_down_w = jnp.einsum("rf,rd->fd", hidden, cotangent, preferred_element_type=jnp.float32)

time: 1350 us -> 1310 us (0.970)
  waiting for transfers between devices: 976 us -> 848 us
  blocking collectives: 41.4 us -> 91.9 us
  starting transfers between devices: 8.72 us -> 26.3 us
    all_gather x1 -> x0, waiting for transfers between devices: 74.1 us -> none  [on_device(): cotangent = lax.all_gather(out_grad, 'tp', axis=1, tiled=True)]
    ppermute x0 -> x3, waiting for transfers between devices: none -> 51.8 us  [wrap_targets(): heard = ppermute(heard, 'tp', current_block)]
    all_gather x1, waiting for transfers between devices: 50.9 us -> 0.01 us  [on_device(): lax.all_gather(residual, 'tp', axis=1, tiled=True)]
    all_gather x1, blocking collectives: 15.1 us -> 65.7 us  [on_device(): lax.all_gather(norm_stack, 'tp', axis=1, tiled=True)]
    all_gather x1, waiting for transfers between devices: 41.3 us -> 0.02 us  [on_device(): lax.all_gather(qkv_weight, ('fsdp', 'ctx'), axis=0, tiled=True)]
    dot_general x1, matrix products: 14.9 us -> 34.1 us  [on_device(): jnp.dot(ffn_in, up_full, preferred_element_type=jnp.float32)]
    ppermute x0 -> x3, starting transfers between devices: none -> 18.9 us  [wrap_targets(): heard = ppermute(heard, 'tp', current_block)]
    unnamed x103 -> x112, local copies, waits for them, and re-layouts: 15.9 us -> 28.7 us
  transfers between devices with their start and end apart: 16 -> 18, of which waited for: 8 -> 6; matrix products, arithmetic and copies ran while one was open for 22% -> 23% of each run, Pallas kernels for 0% -> 0%
where the time goes in v1:
time: 1310 us; the launch traced here: 1300 us
  waiting for transfers between devices  848 us (65%)
  matrix products  204 us (16%)
  blocking collectives  91.9 us (7%)
  other arithmetic  58.8 us (4%)
  local copies, waits for them, and re-layouts  56.3 us (4%)
  starting transfers between devices  26.3 us (2%)
  between operations  15.2 us (1%)
    psum x1, waiting for transfers between devices, on_device(): total_attn, total_ffn = lax.psum((grad_attn_in, grad_ffn_in), 'tp')  563 us
    reduce_scatter x1, waiting for transfers between devices, on_device(): lax.psum_scatter(partial_out, 'tp', scatter_dimension=1, tiled=True)  105 us
    reduce_scatter x1, waiting for transfers between devices, on_device(): lax.psum_scatter(grad_up_w.astype(jnp.bfloat16), ('fsdp', 'ctx'), scatter...  72.4 us
    all_gather x1, blocking collectives, on_device(): lax.all_gather(norm_stack, 'tp', axis=1, tiled=True)  65.7 us
    reduce_scatter x1, waiting for transfers between devices, on_device(): lax.psum_scatter(grad_down_w.astype(jnp.bfloat16), ('fsdp', 'ctx'), scatt...  53.2 us
    ppermute x3, waiting for transfers between devices, wrap_targets(): heard = ppermute(heard, 'tp', current_block)  51.8 us
    dot_general x1, matrix products, on_device(): jnp.dot(ffn_in, up_full, preferred_element_type=jnp.float32)  34.1 us
    unnamed x112, local copies, waits for them, and re-layouts  28.7 us
  transfers between devices with their start and end apart: 18, of which 6 were waited for; matrix products, arithmetic and copies ran while one was open for 23% of the time, Pallas kernels for 0%

profile of v1, /device:TPU:0, one launch (start us, length us, event | category | flops | bytes accessed | tf_op | source)
XLA Modules:
  0.0 1300.8 jit_solution(5261138258798441410)
XLA Ops:
  10.0 3.1 collective-permute-start.2
  18.6 34.0 %collective-permute-done.2 = bf16[1024,512]{1,0:T(8,128)(2,1)S(1)} collective-permute-done((bf16[1024,512]{1,0:T(8,128)(2,1)}, bf16[1024,512]{1,0:T(8,128)(2,1)S(1)}, u32[]{:S(2)}, u32[]{:S(2)}) %collective-permute-start.2) | collective-permute-done | bytes 1048608 | tf_op jit(solution)/shard_map/ppermute | solution.py:24
  52.6 14.3 %collective-permute-start.3 = (bf16[1024,512]{1,0:T(8,128)(2,1)S(1)}, bf16[1024,512]{1,0:T(8,128)(2,1)}, u32[]{:S(2)}, u32[]{:S(2)}) collective-permute-start(bf16[1024,512]{1,0:T(8,128)(2,1)S(1)} %collective-permute-done.2), channel_id=1, source_target_pairs={{0,1},{1,2},{2,3},{3,0},{4,5},{5,6},{6,7},{7,4},{8,9},{9,10},{10,1... | collective-permute-start | bytes 3145736 | tf_op jit(solution)/shard_map/ppermute | solution.py:24
  68.3 65.7 %all_gather.19 = bf16[4,2048]{1,0:T(4,128)(2,1)S(1)} all-gather(bf16[4,512]{1,0:T(4,128)(2,1)S(1)} %pad_maximum_fusion.16), channel_id=1, replica_groups=mesh['fsdp'=4,'ctx'=2,'tp'=4] {'tp'}, dimensions={1}, use_global_device_ids=true | all-gather | bytes 20480 | tf_op jit(solution)/shard_map/all_gather | solution.py:111
  144.2 17.7 %collective-permute-done.4 = bf16[1024,512]{1,0:T(8,128)(2,1)} collective-permute-done((bf16[1024,512]{1,0:T(8,128)(2,1)}, bf16[1024,512]{1,0:T(8,128)(2,1)}, u32[]{:S(2)}, u32[]{:S(2)}) %collective-permute-start.4) | collective-permute-done | bytes 1048608 | tf_op jit(solution)/shard_map/ppermute | solution.py:24
  175.6 3.0 convert_reduce_fusion
  180.4 12.6 convolution_add_fusion
  193.0 6.6 copy.87
  199.6 4.9 fusion.84
  210.0 3.4 subtract_convert_fusion
  217.6 5.2 fusion.39
  228.2 3.5 fusion.90
  232.9 4.0 fusion.89
  250.8 3.1 fusion.17
  258.3 5.3 bitcast_add_fusion.1
  273.7 6.0 convolution_convert_fusion.3
  296.4 3.1 copy.105
  299.5 13.6 %convolution_convert_fusion.2 = bf16[2048,1536]{1,0:T(8,128)(2,1)} fusion(bf16[1024,1536]{0,1:T(8,128)(2,1)} %bitcast.82, bf16[1024,2048]{1,0:T(8,128)(2,1)} %all-gather.6.cloned.1.call-done, f32[2048]{0:T(1024)S(1)} %bitcast.97, f32[2048]{0:T(1024)S(1)} %bitcast.85, f32[1024]{0:T(1024)S(1)} %add_rsqrt_fusion, f32[1024]{0:T(1024)S(1)} %broadcast_multiply_fusion.6), kind=kOutput, calls=%fused_computation.37 | convolution fusion | flops 6458179584 | bytes 13656064 | tf_op jit(solution)/shard_map/rd,rf->df/dot_general | solution.py:266
  313.9 34.1 %multiply_convert_fusion.1 = (bf16[1024,2048]{1,0:T(8,128)(2,1)S(1)}, f32[1024,2048]{1,0:T(8,128)}, f32[1024,2048]{1,0:T(8,128)}) fusion(f32[2048]{0:T(1024)S(1)} %convert_element_type.150, bf16[2048,2048]{1,0:T(8,128)(2,1)} %all-gather.12.cloned.1.call-done, bf16[1024,2048]{1,0:T(8,128)(2,1)} %all-gather.6.cloned.1.call-done, f32[2048]{0:T(1024)S(1)} %bitcast.94, ...), kind=kOutput, calls=%fused_computation.16 | convolution fusion | flops 8740929536 | bytes 33587200 | tf_op jit(solution)/shard_map/dot_general | solution.py:188
  350.0 13.7 %convolution_convert_fusion = bf16[2048,2048]{1,0:T(8,128)(2,1)} fusion(bf16[1024,2048]{1,0:T(8,128)(2,1)S(1)} %get-tuple-element.100, bf16[1024,4096]{1,0:T(8,128)(2,1)} %constant_dynamic-update-slice_fusion, s32[]{:T(128)S(6)} %select_n.39), kind=kOutput, calls=%fused_computation.35 | convolution fusion | flops 8594128896 | bytes 16777220 | tf_op jit(solution)/shard_map/rf,rd->fd/dot_general | solution.py:206
  363.8 20.3 %convert_reduce_fusion.1 = (f32[2048]{0:T(1024)S(1)}, bf16[1024,2048]{1,0:T(8,128)(2,1)}) fusion(f32[1024,2048]{1,0:T(8,128)} %get-tuple-element.101, bf16[2048,2048]{1,0:T(8,128)(2,1)} %all-gather.14.cloned.1.call-done, bf16[1024,4096]{1,0:T(8,128)(2,1)} %constant_dynamic-update-slice_fusion, s32[]{:T(128)S(6)} %select_n.39, ...), kind=kOutput, calls=%fused_computation.7 | convolution fusion | flops 8625584128 | bytes 33570820 | tf_op jit(solution)/shard_map/rd,fd->rf/dot_general | solution.py:210
  384.2 14.1 %convolution_convert_fusion.1 = bf16[2048,2048]{1,0:T(8,128)(2,1)} fusion(bf16[1024,2048]{1,0:T(8,128)(2,1)} %get-tuple-element.150, bf16[1024,2048]{1,0:T(8,128)(2,1)S(1)} %copy-done.1, f32[2048]{0:T(1024)S(1)} %bitcast.95, f32[2048]{0:T(1024)S(1)} %bitcast.88, f32[1024]{0:T(1024)S(1)} %add_rsqrt_fusion, f32[1024]{0:T(1024)S(1)} %broadcast_multiply_fusion.6), kind=kOutput, calls=%fused_computation.36 | convolution fusion | flops 8606711808 | bytes 16801792 | tf_op jit(solution)/shard_map/rd,rf->df/dot_general | solution.py:212
  400.3 11.3 fusion.92
  411.6 13.4 %fusion.93 = f32[1024,2048]{1,0:T(8,128)} fusion(bf16[1024,2048]{1,0:T(8,128)(2,1)S(1)} %copy-done.50, bf16[2048,2048]{1,0:T(8,128)(2,1)} %all-gather.12.cloned.1.call-done), kind=kOutput, calls=%fused_computation.196 | convolution fusion | flops 8589934592 | bytes 20971520 | tf_op jit(solution)/shard_map/rf,df->rd/dot_general | solution.py:214
  425.0 13.0 fusion.91
  438.0 7.1 convolution_add_fusion.1
  450.3 53.2 %reduce-scatter.14.cloned.1.call-done = bf16[2048,256]{1,0:T(8,128)(2,1)} async-done(((bf16[2048,2048]{1,0:T(8,128)(2,1)}), bf16[2048,256]{1,0:T(8,128)(2,1)}) %reduce-scatter.14.cloned.1.call-update) | async-done | bytes 1048592 | tf_op jit(solution)/shard_map/reduce_scatter | solution.py:306
  506.2 72.4 %reduce-scatter.12.cloned.1.call-done = bf16[256,2048]{1,0:T(8,128)(2,1)} async-done(((bf16[2048,2048]{1,0:T(8,128)(2,1)}), bf16[256,2048]{1,0:T(8,128)(2,1)}) %reduce-scatter.12.cloned.1.call-update) | async-done | bytes 1048592 | tf_op jit(solution)/shard_map/reduce_scatter | solution.py:298
  581.4 563.0 %all-reduce.12.cloned.1.call-done = (f32[1024,2048]{1,0:T(8,128)}, f32[1024,2048]{1,0:T(8,128)}) async-done(((f32[1024,2048]{1,0:T(8,128)}, f32[1024,2048]{1,0:T(8,128)}), (f32[1024,2048]{1,0:T(8,128)}, f32[1024,2048]{1,0:T(8,128)})) %all-reduce.12.cloned.1.call-update) | async-done | bytes 16777232 | tf_op jit(solution)/shard_map/psum | solution.py:271
  1144.5 11.8 fusion.81
  1158.6 26.2 %all-reduce.8 = (f32[4,512]{1,0:T(4,128)S(1)}, f32[1536]{0:T(1024)}, f32[512]{0:T(512)S(1)}, f32[2048]{0:T(1024)}) all-reduce(f32[4,512]{1,0:T(4,128)S(1)} %pad_maximum_fusion.15, f32[1536]{0:T(1024)S(1)} %reduce_sum.200, f32[512]{0:T(512)S(1)} %get-tuple-element.120, ...), channel_id=1, replica_groups=mesh['fsdp'=4,'ctx'=2,'tp'=4] {'fsdp','ctx'}, use_global_device_ids=true, to_apply=%region_23.24 | all-reduce | flops 6144 | bytes 49152 | tf_op jit(solution)/shard_map/psum | solution.py:291
  1185.4 104.9 %reduce-scatter.6.cloned.1.call-done = f32[1024,512]{1,0:T(8,128)} async-done(((f32[1024,2048]{1,0:T(8,128)}), f32[1024,512]{1,0:T(8,128)}) %reduce-scatter.6.cloned.1.call-update) | async-done | bytes 2097168 | tf_op jit(solution)/shard_map/reduce_scatter | solution.py:196
  (232 shorter events, 117.8 us)
Async XLA Ops:
  7.2 168.5 %all-gather.6.cloned.1.call-start = ((), (), s32[]{:S(2)}) async-start(), calls=%async_computation.5 | async-start | bytes 5242880 | tf_op jit(solution)/shard_map/all_gather | solution.py:110
  7.9 132.9 %copy-start.46 = (s32[1,13]{1,0:T(1,128)S(1)}, s32[1,13]{1,0:T(1,128)}, u32[]{:S(2)}) copy-start(s32[1,13]{1,0:T(1,128)} %param.33) | copy-start | bytes 160
  7.9 172.4 %all-gather.8.cloned.1.call-start = ((), (), s32[]{:S(2)}) async-start(), calls=%async_computation.6 | async-start | bytes 7077888 | tf_op jit(solution)/shard_map/all_gather | solution.py:115
  8.7 208.9 %all-gather.10.cloned.1.call-start = ((), (), s32[]{:S(2)}) async-start(), calls=%async_computation.7 | async-start | bytes 2359296 | tf_op jit(solution)/shard_map/all_gather | solution.py:119
  9.4 304.4 %all-gather.12.cloned.1.call-start = ((), (), s32[]{:S(2)}) async-start(), calls=%async_computation.8 | async-start | bytes 9437184 | tf_op jit(solution)/shard_map/all_gather | solution.py:116
  10.0 353.8 %all-gather.14.cloned.1.call-start = ((), (), s32[]{:S(2)}) async-start(), calls=%async_computation.9 | async-start | bytes 9437184 | tf_op jit(solution)/shard_map/all_gather | solution.py:120
  10.0 42.6 %collective-permute-start.2 = (bf16[1024,512]{1,0:T(8,128)(2,1)}, bf16[1024,512]{1,0:T(8,128)(2,1)S(1)}, u32[]{:S(2)}, u32[]{:S(2)}) collective-permute-start(bf16[1024,512]{1,0:T(8,128)(2,1)} %param.30), channel_id=1, source_target_pairs={{0,1},{1,2},{2,3},{3,0},{4,5},{5,6},{6,7},{7,4},{8,9},{9,10},{10,1... | collective-permute-start | bytes 3145736 | tf_op jit(solution)/shard_map/ppermute | solution.py:24
  13.1 432.8 %reduce-scatter.10.cloned.1.call-start = ((), (), s32[]{:S(2)}) async-start(), calls=%async_computation.12 | async-start | bytes 2359296 | tf_op jit(solution)/shard_map/reduce_scatter | solution.py:303
  52.6 84.7 %collective-permute-start.3 = (bf16[1024,512]{1,0:T(8,128)(2,1)S(1)}, bf16[1024,512]{1,0:T(8,128)(2,1)}, u32[]{:S(2)}, u32[]{:S(2)}) collective-permute-start(bf16[1024,512]{1,0:T(8,128)(2,1)S(1)} %collective-permute-done.2), channel_id=1, source_target_pairs={{0,1},{1,2},{2,3},{3,0},{4,5},{5,6},{6,7},{7,4},{8,9},{9,10},{10,1... | collective-permute-start | bytes 3145736 | tf_op jit(solution)/shard_map/ppermute | solution.py:24
  137.4 24.5 %collective-permute-start.4 = (bf16[1024,512]{1,0:T(8,128)(2,1)}, bf16[1024,512]{1,0:T(8,128)(2,1)}, u32[]{:S(2)}, u32[]{:S(2)}) collective-permute-start(bf16[1024,512]{1,0:T(8,128)(2,1)} %collective-permute-done.3), channel_id=1, source_target_pairs={{0,1},{1,2},{2,3},{3,0},{4,5},{5,6},{6,7},{7,4},{8,9},{9,10},{10,1... | collective-permute-start | bytes 3145736 | tf_op jit(solution)/shard_map/ppermute | solution.py:24
  140.8 69.2 %copy-start.15 = (f32[1024,32]{1,0:T(8,128)}, f32[1024,32]{1,0:T(8,128)S(1)}, u32[]{:S(2)}) copy-start(f32[1024,32]{1,0:T(8,128)S(1)} %get-tuple-element.136) | copy-start | bytes 393220
  140.8 69.2 %copy-start.17 = (f32[1024,32]{1,0:T(8,128)}, f32[1024,32]{1,0:T(8,128)S(1)}, u32[]{:S(2)}) copy-start(f32[1024,32]{1,0:T(8,128)S(1)} %get-tuple-element.137) | copy-start | bytes 393220
  140.8 26.8 %copy-start.11 = (bf16[1024,512]{1,0:T(8,128)(2,1)S(1)}, bf16[1024,512]{1,0:T(8,128)(2,1)}, u32[]{:S(2)}) copy-start(bf16[1024,512]{1,0:T(8,128)(2,1)} %param.30) | copy-start | bytes 3145732
  144.2 155.4 %copy-start.37 = (f32[1,2048]{1,0:T(1,128)}, f32[1,2048]{1,0:T(1,128)S(1)}, u32[]{:S(2)}) copy-start(f32[1,2048]{1,0:T(1,128)S(1)} %get-tuple-element.128) | copy-start | bytes 24580
  215.3 12.8 collective-permute-start.1
  225.4 20.3 %collective-permute-start = (bf16[1024,2,256]{0,2,1:T(8,128)(2,1)S(1)}, bf16[1024,2,256]{0,2,1:T(8,128)(2,1)S(1)}, u32[]{:S(2)}, u32[]{:S(2)}) collective-permute-start(bf16[1024,2,256]{0,2,1:T(8,128)(2,1)S(1)} %fusion.53), channel_id=1, source_target_pairs={{0,4},{1,5},{2,6},{3,7},{8,12},{9,13},{10,14},{11,15},{16,20},{17,... | collective-permute-start | bytes 3145736 | tf_op jit(solution)/shard_map/ppermute | solution.py:38
  228.1 21.0 %copy-start.23 = (bf16[1024,2,256]{2,0,1:T(8,128)(2,1)}, bf16[1024,2,256]{2,0,1:T(8,128)(2,1)S(1)}, u32[]{:S(2)}) copy-start(bf16[1024,2,256]{2,0,1:T(8,128)(2,1)S(1)} %pad_maximum_fusion.10) | copy-start | bytes 3145732
  244.2 48.7 %collective-permute-start.6 = (f32[1024,2,256]{2,0,1:T(8,128)}, f32[1024,2,256]{2,0,1:T(8,128)}, u32[]{:S(2)}, u32[]{:S(2)}) collective-permute-start(f32[1024,2,256]{2,0,1:T(8,128)} %slice.263), channel_id=1, source_target_pairs={{4,0},{5,1},{6,2},{7,3},{12,8},{13,9},{14,10},{15,11},{20,16},{21,... | collective-permute-start | bytes 6291464 | tf_op jit(solution)/shard_map/ppermute | solution.py:38
  267.1 19.6 %collective-permute-start.5 = (f32[1024,2,256]{2,0,1:T(8,128)}, f32[1024,2,256]{2,0,1:T(8,128)}, u32[]{:S(2)}, u32[]{:S(2)}) collective-permute-start(f32[1024,2,256]{2,0,1:T(8,128)} %slice.261), channel_id=1, source_target_pairs={{4,0},{5,1},{6,2},{7,3},{12,8},{13,9},{14,10},{15,11},{20,16},{21,... | collective-permute-start | bytes 6291464 | tf_op jit(solution)/shard_map/ppermute | solution.py:38
  279.8 168.0 %reduce-scatter.8.cloned.1.call-start = ((), (), s32[]{:S(2)}) async-start(), calls=%async_computation.11 | async-start | bytes 7077888 | tf_op jit(solution)/shard_map/reduce_scatter | solution.py:295
  313.2 190.3 %reduce-scatter.14.cloned.1.call-start = ((), (), s32[]{:S(2)}) async-start(), calls=%async_computation.14 | async-start | bytes 9437184 | tf_op jit(solution)/shard_map/reduce_scatter | solution.py:306
  363.7 214.9 %reduce-scatter.12.cloned.1.call-start = ((), (), s32[]{:S(2)}) async-start(), calls=%async_computation.13 | async-start | bytes 9437184 | tf_op jit(solution)/shard_map/reduce_scatter | solution.py:298
  363.8 20.4 %copy-start.1 = (bf16[1024,2048]{1,0:T(8,128)(2,1)S(1)}, bf16[1024,2048]{1,0:T(8,128)(2,1)}, u32[]{:S(2)}) copy-start(bf16[1024,2048]{1,0:T(8,128)(2,1)} %all-gather.6.cloned.1.call-done) | copy-start | bytes 12582916
  398.3 746.2 %all-reduce.12.cloned.1.call-start = ((), (), s32[]{:S(2)}) async-start(), calls=%async_computation.15 | async-start | bytes 33554432 | tf_op jit(solution)/shard_map/psum | solution.py:271
  400.3 11.3 copy-start.50
  425.0 13.1 %copy-start.14 = (bf16[1024,2,256]{0,2,1:T(8,128)(2,1)S(1)}, bf16[1024,2,256]{0,2,1:T(8,128)(2,1)}, u32[]{:S(2)}) copy-start(bf16[1024,2,256]{0,2,1:T(8,128)(2,1)} %copy-done.13) | copy-start | bytes 3145732
  425.0 13.1 %copy-start.36 = (bf16[512,2048]{1,0:T(8,128)(2,1)S(1)}, bf16[512,2048]{1,0:T(8,128)(2,1)}, u32[]{:S(2)}) copy-start(bf16[512,2048]{1,0:T(8,128)(2,1)} %all-gather.10.cloned.1.call-done) | copy-start | bytes 6291460
  425.0 865.3 %reduce-scatter.6.cloned.1.call-start = ((), (), s32[]{:S(2)}) async-start(), calls=%async_computation.10 | async-start | bytes 10485760 | tf_op jit(solution)/shard_map/reduce_scatter | solution.py:196
  445.2 699.2 %copy-start.38 = (f32[1,2048]{1,0:T(1,128)S(1)}, f32[1,2048]{1,0:T(1,128)}, u32[]{:S(2)}) copy-start(f32[1,2048]{1,0:T(1,128)} %copy-done.37) | copy-start | bytes 24580
  1144.5 12.2 copy-start.12
  1156.2 134.1 %copy-start.19 = (bf16[1024,512]{1,0:T(8,128)(2,1)S(1)}, bf16[1024,512]{1,0:T(8,128)(2,1)}, u32[]{:S(2)}) copy-start(bf16[1024,512]{1,0:T(8,128)(2,1)} %param.29) | copy-start | bytes 3145732
  1184.8 109.0 %copy-start.43 = (f32[512]{0:T(512)}, f32[512]{0:T(512)S(1)}, u32[]{:S(2)}) copy-start(f32[512]{0:T(512)S(1)} %get-tuple-element.180) | copy-start | bytes 6148
  (37 other events, 120.6 us)
Sparse Core Ops, SparseCore 0:
  9.6 119.3 all-gather.5
  130.9 43.8 all-gather.7
  176.7 28.1 all-gather.9
  206.6 54.3 all-gather.11
  262.8 55.9 all-gather.13
  321.9 41.2 reduce-scatter.9
  366.9 61.7 reduce-scatter.7
  432.2 71.2 reduce-scatter.13
  507.4 71.2 reduce-scatter.11
  581.1 563.2 all-reduce.11
  1146.8 143.4 reduce-scatter.5
